TPU v7x, 32 devices: a whole 2x2x4 slice. The times are simulated.
32 devices in a mesh: grp: 2 (over x), tile: 16 (over z, y, core).
Axes of the slice: x: 2, y: 2, z: 4, core: 2. Of those that a mesh axis runs over, the one named last changes fastest.
Arguments:
- features: bfloat16 [384, 64, 2048], P('tile', 'grp'), may hold values from -6 to 6
- occupancy: int32 [192, 2, 16], P('tile', 'grp'), may hold values 0 or 1
- link_weights: int32 [4, 384, 64], P(None, 'tile', 'grp'), may hold values from 0 to 3
- basis_cols: bfloat16 [2048, 256], replicated, may hold values from -0.125 to 0.125
Outputs:
- product: float32 [2048, 256], P('tile')
All inputs are finite; a program needn't handle non-finite values. No bound on the sum of `occupancy` on one device may be relied on, other than what follows from the above.
Results may differ from a plain program's by a relative error of at most 0.004.
Values may be sent and summed in bfloat16 or wider, within the bound.
No kernel may reach another device: no remote copies, remote signals or barrier semaphores. Data moves between devices by JAX's collectives and lax.ppermute only.
A program may use at most 64 MiB of HBM per device.

v0:
```python
import math
import jax
import jax.numpy as jnp
from jax import lax
from jax.sharding import PartitionSpec as P


def extended(cells, sides, width):
    for axis, dim in sides:
        count = lax.axis_size(axis)
        ends = count - 1
        head = lax.slice_in_dim(cells, 0, width, axis=dim)
        tail = lax.slice_in_dim(cells, cells.shape[dim] - width, cells.shape[dim], axis=dim)
        cells = jnp.concatenate(
            [
                lax.ppermute(tail, axis, [(i, (i + 1) % count) for i in range(ends)]),
                cells,
                lax.ppermute(head, axis, [((i + 1) % count, i) for i in range(ends)]),
            ],
            axis=dim,
        )
    return cells


def apply_mask(feat_rows, mask_rows):
    lat_rows, lon_cols, word_count = feat_rows.shape
    groups = mask_rows.shape[1]
    word_blocks = mask_rows.shape[2]
    shaped = feat_rows.reshape(
        lat_rows // 2, 2, groups, lon_cols // groups, word_blocks, word_count // word_blocks
    )
    gate = mask_rows.astype(jnp.bfloat16)[:, None, :, None, :, None]
    return (shaped * gate).reshape(lat_rows * lon_cols, word_count)


def spatial_average(padded, link_weights):
    weights = link_weights.astype(jnp.float32)
    north_side = padded[:-2, 1:-1].astype(jnp.float32)
    south_side = padded[2:, 1:-1].astype(jnp.float32)
    west_side = padded[1:-1, :-2].astype(jnp.float32)
    east_side = padded[1:-1, 2:].astype(jnp.float32)
    weighted = weights[0][:, :, None] * north_side + weights[1][:, :, None] * south_side
    weighted = weighted + weights[2][:, :, None] * west_side + weights[3][:, :, None] * east_side
    weight_total = jnp.maximum(jnp.sum(weights, axis=0), 1.0)
    return (weighted / weight_total[:, :, None]).astype(jnp.bfloat16)


def per_device(features, occupancy, link_weights, basis_cols):
    lat_rows, lon_cols, word_count = features.shape
    rank_width = basis_cols.shape[1]
    masked = apply_mask(features, occupancy)
    projected = jnp.dot(masked, basis_cols, preferred_element_type=jnp.float32).astype(jnp.bfloat16)
    projected = projected.reshape(lat_rows, lon_cols, rank_width)
    padded = extended(projected, (("grp", 1), ("tile", 0)), 1)
    smooth = spatial_average(padded, link_weights).reshape(lat_rows * lon_cols, rank_width)
    scaling = 1.0 / math.sqrt(lat_rows * lon_cols * lax.axis_size("grp") * lax.axis_size("tile"))
    share_rows = word_count // lax.axis_size("tile")
    local_term = lax.dot_general(
        masked, smooth, (((0,), (0,)), ((), ())), preferred_element_type=jnp.float32
    )
    summed = lax.psum(local_term, ("grp", "tile"))
    own_rows = lax.dynamic_slice_in_dim(summed, lax.axis_index("tile") * share_rows, share_rows, 0)
    return own_rows * scaling


def solution(mesh):
    placed = (P("tile", "grp", None), P("tile", "grp", None), P(None, "tile", "grp"), P())
    return jax.shard_map(
        per_device, mesh=mesh, in_specs=placed, out_specs=P("tile", None), check_vma=False
    )
```

profile of v0, /device:TPU:0, one launch (start us, length us, event | category | flops | bytes accessed | tf_op | source)
XLA Modules:
  0.0 175.5 jit_solution(12780380878305803182)
XLA Ops:
  6.5 0.0 copy-start
  6.5 0.0 all-reduce.2.cloned.1.call-start
  6.5 0.0 copy-start.2
  6.5 0.8 convert_element_type.24
  7.4 0.5 mul.80
  7.9 0.0 copy-done
  7.9 0.9 copy-done.2
  8.8 0.0 copy-start.1
  8.8 1.0 fusion.8
  9.8 4.9 %collective-permute-start = (bf16[24,1,256]{2,1,0:T(2,128)(2,1)S(1)}, bf16[24,1,256]{2,1,0:T(2,128)(2,1)S(1)}, u32[]{:S(2)}, u32[]{:S(2)}) collective-permute-start(bf16[24,1,256]{2,1,0:T(2,128)(2,1)S(1)} %get-tuple-element.7), channel_id=1, source_target_pairs={{0,16},{1,17},{2,18},{3,19},{4,20},{5,21},{6,22},{7,23},{8,24},{9,... | collective-permute-start | bytes 36872 | tf_op jit(solution)/shard_map/ppermute | solution.py:16
  14.7 1.3 collective-permute-start.1
  16.0 0.0 copy-done.1
  16.1 0.1 collective-permute-done
  16.2 4.2 %collective-permute-done.1 = bf16[24,1,256]{2,1,0:T(2,128)(2,1)S(1)} collective-permute-done((bf16[24,1,256]{2,1,0:T(2,128)(2,1)S(1)}, bf16[24,1,256]{2,1,0:T(2,128)(2,1)S(1)}, u32[]{:S(2)}, u32[]{:S(2)}) %collective-permute-start.1) | collective-permute-done | bytes 12320 | tf_op jit(solution)/shard_map/ppermute | solution.py:18
  20.5 1.3 collective-permute-start.2
  21.8 1.3 collective-permute-start.3
  23.1 0.1 mul.74
  23.2 0.0 collective-permute-done.2
  23.2 3.4 %collective-permute-done.3 = bf16[1,34,256]{2,1,0:T(8,128)(2,1)S(1)} collective-permute-done((bf16[1,34,256]{2,1,0:T(8,128)(2,1)S(1)}, bf16[1,34,256]{2,1,0:T(8,128)(2,1)S(1)}, u32[]{:S(2)}, u32[]{:S(2)}) %collective-permute-start.3) | collective-permute-done | bytes 17440 | tf_op jit(solution)/shard_map/ppermute | solution.py:18
  26.6 3.2 %fusion.4 = f32[2048,256]{1,0:T(8,128)} fusion(bf16[24,32,2048]{2,1,0:T(8,128)(2,1)S(1)} %copy-done.2, bf16[24,2048]{1,0:T(8,128)(2,1)S(1)} %bitcast.34, bf16[24,1,256]{2,1,0:T(2,128)(2,1)S(1)} %collective-permute-done.1, bf16[24,32,256]{2,1,0:T(8,128)(2,1)S(1)} %bitcast.32, bf16[24,1,256]{2,1,0:T(2,128)(2,1)S(1)} %collective-permute-done, ...), kind=kOutput, calls=%fused_computation.5 | convolution fusion | flops 813367296 | bytes 5809152 | tf_op jit(solution)/shard_map/dot_general | solution.py:58
  29.8 0.0 all-reduce.2.cloned.1.call-update
  29.8 137.3 %all-reduce.2.cloned.1.call-done = f32[2048,256]{1,0:T(8,128)} async-done(((f32[2048,256]{1,0:T(8,128)}), f32[2048,256]{1,0:T(8,128)}) %all-reduce.2.cloned.1.call-update) | async-done | bytes 2097168 | tf_op jit(solution)/shard_map/psum | solution.py:61
  167.1 1.6 dynamic-slice_multiply_fusion
  (8 shorter events, 0.1 us)
Async XLA Ops:
  6.5 1.3 copy-start
  6.5 160.6 %all-reduce.2.cloned.1.call-start = ((), (), s32[]{:S(2)}) async-start(), calls=%async_computation | async-start | bytes 4194304 | tf_op jit(solution)/shard_map/psum | solution.py:61
  6.5 2.2 %copy-start.2 = (bf16[24,32,2048]{2,1,0:T(8,128)(2,1)S(1)}, bf16[24,32,2048]{2,1,0:T(8,128)(2,1)}, u32[]{:S(2)}) copy-start(bf16[24,32,2048]{2,1,0:T(8,128)(2,1)} %param.4) | copy-start | bytes 9437188
  8.8 7.3 %copy-start.1 = (s32[4,24,32]{2,1,0:T(8,128)S(1)}, s32[4,24,32]{2,1,0:T(8,128)}, u32[]{:S(2)}) copy-start(s32[4,24,32]{2,1,0:T(8,128)} %param.6) | copy-start | bytes 36868
  9.8 6.4 %collective-permute-start = (bf16[24,1,256]{2,1,0:T(2,128)(2,1)S(1)}, bf16[24,1,256]{2,1,0:T(2,128)(2,1)S(1)}, u32[]{:S(2)}, u32[]{:S(2)}) collective-permute-start(bf16[24,1,256]{2,1,0:T(2,128)(2,1)S(1)} %get-tuple-element.7), channel_id=1, source_target_pairs={{0,16},{1,17},{2,18},{3,19},{4,20},{5,21},{6,22},{7,23},{8,24},{9,... | collective-permute-start | bytes 36872 | tf_op jit(solution)/shard_map/ppermute | solution.py:16
  14.7 5.7 %collective-permute-start.1 = (bf16[24,1,256]{2,1,0:T(2,128)(2,1)S(1)}, bf16[24,1,256]{2,1,0:T(2,128)(2,1)S(1)}, u32[]{:S(2)}, u32[]{:S(2)}) collective-permute-start(bf16[24,1,256]{2,1,0:T(2,128)(2,1)S(1)} %get-tuple-element.8), channel_id=1, source_target_pairs={{16,0},{17,1},{18,2},{19,3},{20,4},{21,5},{22,6},{23,7},{24,8},{25... | collective-permute-start | bytes 36872 | tf_op jit(solution)/shard_map/ppermute | solution.py:18
  20.5 2.7 %collective-permute-start.2 = (bf16[1,34,256]{2,1,0:T(8,128)(2,1)S(1)}, bf16[1,34,256]{2,1,0:T(8,128)(2,1)S(1)}, u32[]{:S(2)}, u32[]{:S(2)}) collective-permute-start(bf16[1,34,256]{2,1,0:T(8,128)(2,1)S(1)} %get-tuple-element.5), channel_id=1, source_target_pairs={{0,1},{1,2},{2,3},{3,4},{4,5},{5,6},{6,7},{7,8},{8,9},{9,10},{10,1... | collective-permute-start | bytes 52232 | tf_op jit(solution)/shard_map/ppermute | solution.py:16
  21.8 4.8 %collective-permute-start.3 = (bf16[1,34,256]{2,1,0:T(8,128)(2,1)S(1)}, bf16[1,34,256]{2,1,0:T(8,128)(2,1)S(1)}, u32[]{:S(2)}, u32[]{:S(2)}) collective-permute-start(bf16[1,34,256]{2,1,0:T(8,128)(2,1)S(1)} %get-tuple-element.6), channel_id=1, source_target_pairs={{1,0},{2,1},{3,2},{4,3},{5,4},{6,5},{7,6},{8,7},{9,8},{10,9},{11,1... | collective-permute-start | bytes 52232 | tf_op jit(solution)/shard_map/ppermute | solution.py:18
Sparse Core Ops, SparseCore 0:
  29.9 137.1 all-reduce.1
where the time goes:
time: 176 us
  waiting for transfers between devices  145 us (82%)
  between operations  13.5 us (8%)
  starting transfers between devices  8.75 us (5%)
  matrix products  4.18 us (2%)
  other arithmetic  2.46 us (1%)
    psum x1, waiting for transfers between devices, per_device(): summed = lax.psum(local_term, ('grp', 'tile'))  137 us
    ppermute x2, waiting for transfers between devices, extended(): lax.ppermute(head, axis, [((i + 1) % count, i) for i in range(ends)])  7.61 us
    ppermute x2, starting transfers between devices, extended(): lax.ppermute(tail, axis, [(i, (i + 1) % count) for i in range(ends)])  6.16 us
  transfers between devices with their start and end apart: 5, of which 4 were waited for; matrix products, arithmetic and copies ran while one was open for 0% of the time, Pallas kernels for 0%

commit v1 on v0

--- a/solution.py
+++ b/solution.py
@@ -58,7 +58,8 @@
     local_term = lax.dot_general(
         masked, smooth, (((0,), (0,)), ((), ())), preferred_element_type=jnp.float32
     )
-    summed = lax.psum(local_term, ("grp", "tile"))
+    inner = lax.psum(local_term, "grp")
+    summed = lax.psum(inner, "tile")
     own_rows = lax.dynamic_slice_in_dim(summed, lax.axis_index("tile") * share_rows, share_rows, 0)
     return own_rows * scaling
 

time: 176 us -> 206 us (1.17)
  waiting for transfers between devices: 145 us -> 175 us
    psum x1 -> x2, waiting for transfers between devices: 137 us -> 167 us  [the longest x1 102 us: per_device(): summed = lax.psum(inner, 'tile')]
  transfers between devices with their start and end apart: 5 -> 6, of which waited for: 4 -> 5; matrix products, arithmetic and copies ran while one was open for 0% -> 0% of each run, Pallas kernels for 0% -> 0%
where the time goes in v1:
time: 206 us; the launch traced here: 205 us
  waiting for transfers between devices  175 us (85%)
  between operations  13.5 us (7%)
  starting transfers between devices  8.79 us (4%)
  matrix products  4.18 us (2%)
  other arithmetic  2.46 us (1%)
    psum x1, waiting for transfers between devices, per_device(): summed = lax.psum(inner, 'tile')  102 us
    psum x1, waiting for transfers between devices, per_device(): inner = lax.psum(local_term, 'grp')  65.4 us
    ppermute x2, waiting for transfers between devices, extended(): lax.ppermute(head, axis, [((i + 1) % count, i) for i in range(ends)])  7.61 us
    ppermute x2, starting transfers between devices, extended(): lax.ppermute(tail, axis, [(i, (i + 1) % count) for i in range(ends)])  6.16 us
  transfers between devices with their start and end apart: 6, of which 5 were waited for; matrix products, arithmetic and copies ran while one was open for 0% of the time, Pallas kernels for 0%

profile of v1, /device:TPU:0, one launch (start us, length us, event | category | flops | bytes accessed | tf_op | source)
XLA Modules:
  0.0 205.5 jit_solution(9749530647385877107)
XLA Ops:
  6.5 0.0 copy-start
  6.5 0.0 all-reduce.3.cloned.1.call-start
  6.5 0.8 convert_element_type.24
  7.4 0.5 mul.80
  7.9 0.0 copy-done
  7.9 0.9 copy-done.2
  8.8 1.0 fusion.8
  9.8 4.9 %collective-permute-start = (bf16[24,1,256]{2,1,0:T(2,128)(2,1)S(1)}, bf16[24,1,256]{2,1,0:T(2,128)(2,1)S(1)}, u32[]{:S(2)}, u32[]{:S(2)}) collective-permute-start(bf16[24,1,256]{2,1,0:T(2,128)(2,1)S(1)} %get-tuple-element.7), channel_id=1, source_target_pairs={{0,16},{1,17},{2,18},{3,19},{4,20},{5,21},{6,22},{7,23},{8,24},{9,... | collective-permute-start | bytes 36872 | tf_op jit(solution)/shard_map/ppermute | solution.py:16
  14.7 1.3 collective-permute-start.1
  16.0 0.0 copy-done.1
  16.1 0.1 collective-permute-done
  16.2 4.2 %collective-permute-done.1 = bf16[24,1,256]{2,1,0:T(2,128)(2,1)S(1)} collective-permute-done((bf16[24,1,256]{2,1,0:T(2,128)(2,1)S(1)}, bf16[24,1,256]{2,1,0:T(2,128)(2,1)S(1)}, u32[]{:S(2)}, u32[]{:S(2)}) %collective-permute-start.1) | collective-permute-done | bytes 12320 | tf_op jit(solution)/shard_map/ppermute | solution.py:18
  20.5 1.3 collective-permute-start.2
  21.8 1.3 collective-permute-start.3
  23.1 0.1 mul.74
  23.2 0.0 collective-permute-done.2
  23.2 3.4 %collective-permute-done.3 = bf16[1,34,256]{2,1,0:T(8,128)(2,1)S(1)} collective-permute-done((bf16[1,34,256]{2,1,0:T(8,128)(2,1)S(1)}, bf16[1,34,256]{2,1,0:T(8,128)(2,1)S(1)}, u32[]{:S(2)}, u32[]{:S(2)}) %collective-permute-start.3) | collective-permute-done | bytes 17440 | tf_op jit(solution)/shard_map/ppermute | solution.py:18
  26.6 3.2 %fusion.4 = f32[2048,256]{1,0:T(8,128)} fusion(bf16[24,32,2048]{2,1,0:T(8,128)(2,1)S(1)} %copy-done.2, bf16[24,2048]{1,0:T(8,128)(2,1)S(1)} %bitcast.34, bf16[24,1,256]{2,1,0:T(2,128)(2,1)S(1)} %collective-permute-done.1, bf16[24,32,256]{2,1,0:T(8,128)(2,1)S(1)} %bitcast.32, bf16[24,1,256]{2,1,0:T(2,128)(2,1)S(1)} %collective-permute-done, ...), kind=kOutput, calls=%fused_computation.5 | convolution fusion | flops 813367296 | bytes 5809152 | tf_op jit(solution)/shard_map/dot_general | solution.py:58
  29.8 0.0 all-reduce.3.cloned.1.call-update
  29.8 0.0 all-reduce.5.cloned.1.call-start
  29.8 65.4 %all-reduce.3.cloned.1.call-done = f32[2048,256]{1,0:T(8,128)} async-done(((f32[2048,256]{1,0:T(8,128)}), f32[2048,256]{1,0:T(8,128)}) %all-reduce.3.cloned.1.call-update) | async-done | bytes 2097168 | tf_op jit(solution)/shard_map/psum | solution.py:61
  95.3 0.0 all-reduce.5.cloned.1.call-update
  95.3 101.7 %all-reduce.5.cloned.1.call-done = f32[2048,256]{1,0:T(8,128)} async-done(((f32[2048,256]{1,0:T(8,128)}), f32[2048,256]{1,0:T(8,128)}) %all-reduce.5.cloned.1.call-update) | async-done | bytes 2097168 | tf_op jit(solution)/shard_map/psum | solution.py:62
  197.0 1.6 dynamic-slice_multiply_fusion
  (10 shorter events, 0.1 us)
Async XLA Ops:
  6.5 1.3 copy-start
  6.5 88.7 %all-reduce.3.cloned.1.call-start = ((), (), s32[]{:S(2)}) async-start(), calls=%async_computation | async-start | bytes 4194304 | tf_op jit(solution)/shard_map/psum | solution.py:61
  6.5 2.2 %copy-start.2 = (bf16[24,32,2048]{2,1,0:T(8,128)(2,1)S(1)}, bf16[24,32,2048]{2,1,0:T(8,128)(2,1)}, u32[]{:S(2)}) copy-start(bf16[24,32,2048]{2,1,0:T(8,128)(2,1)} %param.4) | copy-start | bytes 9437188
  8.8 7.3 %copy-start.1 = (s32[4,24,32]{2,1,0:T(8,128)S(1)}, s32[4,24,32]{2,1,0:T(8,128)}, u32[]{:S(2)}) copy-start(s32[4,24,32]{2,1,0:T(8,128)} %param.6) | copy-start | bytes 36868
  9.8 6.4 %collective-permute-start = (bf16[24,1,256]{2,1,0:T(2,128)(2,1)S(1)}, bf16[24,1,256]{2,1,0:T(2,128)(2,1)S(1)}, u32[]{:S(2)}, u32[]{:S(2)}) collective-permute-start(bf16[24,1,256]{2,1,0:T(2,128)(2,1)S(1)} %get-tuple-element.7), channel_id=1, source_target_pairs={{0,16},{1,17},{2,18},{3,19},{4,20},{5,21},{6,22},{7,23},{8,24},{9,... | collective-permute-start | bytes 36872 | tf_op jit(solution)/shard_map/ppermute | solution.py:16
  14.7 5.7 %collective-permute-start.1 = (bf16[24,1,256]{2,1,0:T(2,128)(2,1)S(1)}, bf16[24,1,256]{2,1,0:T(2,128)(2,1)S(1)}, u32[]{:S(2)}, u32[]{:S(2)}) collective-permute-start(bf16[24,1,256]{2,1,0:T(2,128)(2,1)S(1)} %get-tuple-element.8), channel_id=1, source_target_pairs={{16,0},{17,1},{18,2},{19,3},{20,4},{21,5},{22,6},{23,7},{24,8},{25... | collective-permute-start | bytes 36872 | tf_op jit(solution)/shard_map/ppermute | solution.py:18
  20.5 2.7 %collective-permute-start.2 = (bf16[1,34,256]{2,1,0:T(8,128)(2,1)S(1)}, bf16[1,34,256]{2,1,0:T(8,128)(2,1)S(1)}, u32[]{:S(2)}, u32[]{:S(2)}) collective-permute-start(bf16[1,34,256]{2,1,0:T(8,128)(2,1)S(1)} %get-tuple-element.5), channel_id=1, source_target_pairs={{0,1},{1,2},{2,3},{3,4},{4,5},{5,6},{6,7},{7,8},{8,9},{9,10},{10,1... | collective-permute-start | bytes 52232 | tf_op jit(solution)/shard_map/ppermute | solution.py:16
  21.8 4.8 %collective-permute-start.3 = (bf16[1,34,256]{2,1,0:T(8,128)(2,1)S(1)}, bf16[1,34,256]{2,1,0:T(8,128)(2,1)S(1)}, u32[]{:S(2)}, u32[]{:S(2)}) collective-permute-start(bf16[1,34,256]{2,1,0:T(8,128)(2,1)S(1)} %get-tuple-element.6), channel_id=1, source_target_pairs={{1,0},{2,1},{3,2},{4,3},{5,4},{6,5},{7,6},{8,7},{9,8},{10,9},{11,1... | collective-permute-start | bytes 52232 | tf_op jit(solution)/shard_map/ppermute | solution.py:18
  29.8 167.3 %all-reduce.5.cloned.1.call-start = ((), (), s32[]{:S(2)}) async-start(), calls=%async_computation.1 | async-start | bytes 4194304 | tf_op jit(solution)/shard_map/psum | solution.py:62
Sparse Core Ops, SparseCore 0:
  29.9 65.3 all-reduce.2
  98.8 98.1 all-reduce.4
